TPU v7x, 512 devices: a whole 4x4x16 slice. The times are simulated.
512 devices in a mesh: dp: 8 (over y, core), tensor: 64 (over z, x).
Axes of the slice: x: 4, y: 4, z: 16, core: 2. Of those that a mesh axis runs over, the one named last changes fastest.
Arguments:
- hidden_states: bfloat16 [8192, 2560], P(('dp', 'tensor')), may hold values from -8 to 8
- norm_gain: float32 [2560], replicated, may hold values from 0.5 to 1.5
- head_weight: bfloat16 [2560, 76032], P('dp', 'tensor'), may hold values from -8 to 8
- targets: int32 [8192], P(('dp', 'tensor')), may hold values from 0 to 76031
- lengths: int32 [8, 16], P('dp'), may hold values from 1 to 512, 1024 in all within a row
Outputs:
- log_prob: float32 [8192], P(('dp', 'tensor'))
- entropy: float32 [8192], P(('dp', 'tensor'))
- seq_mean: float32 [8, 16], P('dp')
Inputs may be any that keep to these rules, and one draw needn't show every extreme that they name: Each data group's lengths sum to 16 * 64.
All inputs are finite; a program needn't handle non-finite values.
Results may differ from a plain program's by a relative error of at most 0.0072.
Values may be sent and summed in bfloat16 or wider, within the bound.
A program may use at most 64 MiB of HBM per device.

v0:
```python
import jax
import jax.numpy as jnp
from jax import lax
from jax.sharding import PartitionSpec as P


def shard_stats(logits, wanted, vocab_start):
    highest = jnp.max(logits, axis=1)
    expo = jnp.exp(logits - highest[:, None])
    totals = jnp.sum(expo, axis=1)
    weighted = jnp.sum(expo * logits, axis=1)
    columns = lax.broadcasted_iota(jnp.int32, logits.shape, 1)
    picked = jnp.sum(jnp.where(columns == (wanted - vocab_start)[:, None], logits, 0.0), axis=1)
    return jnp.stack([highest, totals, weighted, picked])


def by_blocks(work, matrix_rows, wanted):
    row_count = matrix_rows.shape[0]
    block_count = row_count // 512

    def one_block(couple):
        return work(couple[0], couple[1])

    results = lax.map(
        one_block,
        (
            matrix_rows.reshape(block_count, 512, matrix_rows.shape[1]),
            wanted.reshape(block_count, 512),
        ),
    )
    return jnp.transpose(results, (1, 0, 2)).reshape(4, row_count)


def finish_rows(largest, sum_exp, sum_weighted, sum_picked):
    lse = largest + jnp.log(sum_exp)
    return (sum_picked - lse, lse - sum_weighted / sum_exp)


def sequence_sums(values, seq_lengths, seq_count):
    positions = jnp.arange(values.shape[0], dtype=jnp.int32)
    seq_ends = jnp.cumsum(seq_lengths)
    segment = jnp.sum((positions[:, None] >= seq_ends[None, :]).astype(jnp.int32), axis=1)
    onehot = segment[:, None] == jnp.arange(seq_count, dtype=jnp.int32)[None, :]
    return jnp.sum(jnp.where(onehot, values[:, None], 0.0), axis=0)


def on_device(hidden_states, norm_gain, head_weight, targets, lengths):
    widths = hidden_states.astype(jnp.float32)
    meansq = jnp.mean(widths * widths, axis=1, keepdims=True)
    normed = (widths * lax.rsqrt(meansq + 1e-06) * norm_gain).astype(jnp.bfloat16)
    vocab_part = head_weight.shape[1]
    tensor_index = lax.axis_index("tensor")
    vocab_start = tensor_index * vocab_part
    own_rows = hidden_states.shape[0]
    own_start = tensor_index * own_rows
    seq_lengths = lengths[0]
    seq_count = lengths.shape[1]
    wanted_all = lax.all_gather(targets, "tensor", axis=0, tiled=True)
    rows_all = lax.all_gather(normed, "tensor", axis=0, tiled=True)
    logits = jnp.dot(
        rows_all,
        lax.all_gather(head_weight, "dp", axis=0, tiled=True),
        preferred_element_type=jnp.float32,
    )

    def logit_stats(block_logits, block_wanted):
        return shard_stats(block_logits, block_wanted, vocab_start)

    row_table = by_blocks(logit_stats, logits, wanted_all)
    highest = row_table[0]
    totals = row_table[1]
    weighted = row_table[2]
    picked = row_table[3]
    largest = lax.pmax(highest, "tensor")
    factor = jnp.exp(highest - largest)
    sum_exp, sum_weighted, sum_picked = lax.psum(
        (totals * factor, weighted * factor, picked), "tensor"
    )
    group_logprob, group_entropy = finish_rows(largest, sum_exp, sum_weighted, sum_picked)
    sums = sequence_sums(group_logprob, seq_lengths, seq_count)
    log_prob = lax.dynamic_slice_in_dim(group_logprob, own_start, own_rows, 0)
    entropy = lax.dynamic_slice_in_dim(group_entropy, own_start, own_rows, 0)
    seq_mean = (sums / seq_lengths.astype(jnp.float32))[None, :]
    return (log_prob, entropy, seq_mean)


def solution(mesh):
    in_specs = (
        P(("dp", "tensor"), None),
        P(),
        P("dp", "tensor"),
        P(("dp", "tensor")),
        P("dp", None),
    )
    out_specs = (P(("dp", "tensor")), P(("dp", "tensor")), P("dp", None))
    return jax.shard_map(
        on_device, mesh=mesh, in_specs=in_specs, out_specs=out_specs, check_vma=False
    )
```

profile of v0, /device:TPU:8, one launch (start us, length us, event | category | flops | bytes accessed | tf_op | source)
XLA Modules:
  0.0 658.7 jit_solution(5995464024630584219)
XLA Ops:
  7.2 0.0 all-gather.3.cloned.1.call-start
  7.2 1.0 fusion.5
  8.2 1.6 fusion.7
  9.8 0.0 all-gather.3.cloned.1.call-update
  9.9 0.0 all-gather.5.cloned.1.call-start
  9.9 0.7 all-gather.5.cloned.1.call-update
  10.6 1.3 dynamic-slice
  12.6 0.9 dynamic-update-slice
  13.4 34.0 %all-reduce = s32[1024]{0:T(1024)S(1)} all-reduce(s32[1024]{0:T(1024)S(1)} %dynamic-update-slice), channel_id=1, replica_groups=mesh['dp'=8,'tensor'=64] {'tensor'}, use_global_device_ids=true, to_apply=%add | all-reduce | flops 1024 | bytes 8192
  47.5 0.7 copy.13
  48.3 0.1 reduce.1
  48.4 0.1 convert_reduce_fusion
  48.5 116.8 %all-gather.3.cloned.1.call-done = bf16[1024,2560]{1,0:T(8,128)(2,1)} async-done(((bf16[16,2560]{1,0:T(8,128)(2,1)}), bf16[1024,2560]{1,0:T(8,128)(2,1)}) %all-gather.3.cloned.1.call-update) | async-done | bytes 5242896 | tf_op jit(solution)/shard_map/all_gather | solution.py:59
  165.2 45.0 %all-gather.5.cloned.1.call-done = bf16[2560,1188]{1,0:T(8,128)(2,1)} async-done(((bf16[320,1188]{1,0:T(8,128)(2,1)}), bf16[2560,1188]{1,0:T(8,128)(2,1)}) %all-gather.5.cloned.1.call-update) | async-done | bytes 6082576 | tf_op jit(solution)/shard_map/all_gather | solution.py:62
  210.2 12.2 %fusion.12 = f32[1024,1188]{1,0:T(8,128)} fusion(bf16[1024,2560]{1,0:T(8,128)(2,1)} %all-gather.3.cloned.1.call-done, bf16[2560,1188]{1,0:T(8,128)(2,1)} %all-gather.5.cloned.1.call-done), kind=kOutput, calls=%fused_computation.30 | convolution fusion | flops 6228541440 | bytes 16191488 | tf_op jit(solution)/shard_map/while | solution.py:24
  222.4 0.0 copy-start
  222.4 9.5 %while.10 = (s32[]{:T(128)}, f32[2,4,512]{2,1,0:T(4,128)S(1)}, f32[2,512,1188]{2,1,0:T(8,128)}, s32[2,512]{1,0:T(2,128)S(1)}, s32[]{:T(128)}, /*index=5*/s32[]{:T(128)}) while((s32[]{:T(128)}, f32[2,4,512]{2,1,0:T(4,128)S(1)}, f32[2,512,1188]{2,1,0:T(8,128)}, s32[2,512]{1,0:T(2,128)S(1)}, s32[]{:T(128)}, /*index=5*/s32[]{:T(128)}) %tuple.41), condition=%wide.region_6.7_spmd, body=%wide.region_1.6_spmd.sunk | while | flops 4870658 | bytes 4898905 | solution.py:24
  222.4 1.9 dynamic-slice_reduce_fusion.2
  224.4 2.7 fusion.17
  227.2 1.9 dynamic-slice_reduce_fusion.2
  229.1 2.7 fusion.17
  231.9 144.1 %pmax.7 = f32[1024]{0:T(1024)S(1)} all-reduce(f32[1024]{0:T(1024)S(1)} %bitcast.55), channel_id=1, replica_groups=mesh['dp'=8,'tensor'=64] {'tensor'}, use_global_device_ids=true, to_apply=%region_8.9 | all-reduce | flops 1024 | bytes 8192 | tf_op jit(solution)/shard_map/pmax | solution.py:74
  376.1 274.0 %all-reduce.1 = (f32[1024]{0:T(1024)S(1)}, f32[1024]{0:T(1024)S(1)}, f32[1024]{0:T(1024)S(1)}) all-reduce(f32[1024]{0:T(1024)S(1)} %bitcast.58, f32[1024]{0:T(1024)S(1)} %get-tuple-element.69, f32[1024]{0:T(1024)S(1)} %get-tuple-element.68), channel_id=1, replica_groups=mesh['dp'=8,'tensor'=64] {'tensor'}, use_global_device_ids=true, to_apply=%region_7.8 | all-reduce | flops 3072 | bytes 24576 | tf_op jit(solution)/shard_map/psum | solution.py:76
  650.1 0.1 select_reduce_fusion
  650.2 0.0 copy-done
  650.2 0.5 bitcast_divide_fusion
  650.7 0.6 dynamic_slice.14
  651.3 0.6 dynamic_slice.15
  (12 shorter events, 0.2 us)
Async XLA Ops:
  7.2 158.1 %all-gather.3.cloned.1.call-start = ((), (), s32[]{:S(2)}) async-start(), calls=%async_computation | async-start | bytes 5324800 | tf_op jit(solution)/shard_map/all_gather | solution.py:59
  9.9 200.3 %all-gather.5.cloned.1.call-start = ((), (), s32[]{:S(2)}) async-start(), calls=%async_computation.1 | async-start | bytes 7372800 | tf_op jit(solution)/shard_map/all_gather | solution.py:62
  222.4 427.8 %copy-start = (s32[1,16]{1,0:T(1,128)S(1)}, s32[1,16]{1,0:T(1,128)}, u32[]{:S(2)}) copy-start(s32[1,16]{1,0:T(1,128)} %param.11) | copy-start | bytes 196
Sparse Core Ops, SparseCore 0:
  10.9 154.2 all-gather.2
  167.4 42.8 all-gather.4
where the time goes:
time: 659 us
  blocking collectives  452 us (69%)
  waiting for transfers between devices  162 us (25%)
  between operations  14.7 us (2%)
  other arithmetic  13 us (2%)
  matrix products  12.2 us (2%)
    psum x1, blocking collectives, on_device(): lax.psum((totals * factor, weighted * factor, picked), 'tensor')  274 us
    pmax x1, blocking collectives, on_device(): largest = lax.pmax(highest, 'tensor')  144 us
    all_gather x1, waiting for transfers between devices, on_device(): rows_all = lax.all_gather(normed, 'tensor', axis=0, tiled=True)  117 us
    all_gather x1, waiting for transfers between devices, on_device(): lax.all_gather(head_weight, 'dp', axis=0, tiled=True)  45 us
    unnamed x1, blocking collectives  34 us
  transfers between devices with their start and end apart: 2, of which 2 were waited for; matrix products, arithmetic and copies ran while one was open for 0% of the time, Pallas kernels for 0%

commit v1 on v0

--- a/solution.py
+++ b/solution.py
@@ -2,6 +2,28 @@
 import jax.numpy as jnp
 from jax import lax
 from jax.sharding import PartitionSpec as P
+
+
+def in_order(blocks, dim):
+    blocks = jnp.moveaxis(blocks, 0, dim)
+    dims = blocks.shape
+    return blocks.reshape(*dims[:dim], dims[dim] * dims[dim + 1], *dims[dim + 2 :])
+
+
+def ring_gather(x, axis, dim):
+    size = lax.axis_size(axis)
+    pairs = [(i, (i + 1) % size) for i in range(size)]
+    back = [(b, a) for a, b in pairs]
+    lower, upper = ([], [])
+    for lap in range(size - 1):
+        if lap % 2 == 0:
+            lower.append(lax.ppermute(lower[-1] if lower else x, axis, pairs))
+        else:
+            upper.append(lax.ppermute(upper[-1] if upper else x, axis, back))
+    blocks = jnp.stack([*lower[::-1], x, *upper])
+    shift = lax.axis_index(axis) - len(lower)
+    blocks = blocks[(jnp.arange(size) - shift) % size]
+    return in_order(blocks, dim)
 
 
 def shard_stats(logits, wanted, vocab_start):
@@ -58,9 +80,7 @@
     wanted_all = lax.all_gather(targets, "tensor", axis=0, tiled=True)
     rows_all = lax.all_gather(normed, "tensor", axis=0, tiled=True)
     logits = jnp.dot(
-        rows_all,
-        lax.all_gather(head_weight, "dp", axis=0, tiled=True),
-        preferred_element_type=jnp.float32,
+        rows_all, ring_gather(head_weight, "dp", 0), preferred_element_type=jnp.float32
     )
 
     def logit_stats(block_logits, block_wanted):

time: 659 us -> 610 us (0.926)
  waiting for transfers between devices: 162 us -> 95.8 us
  local copies, waits for them, and re-layouts: 4.06 us -> 21.8 us
    all_gather x1, waiting for transfers between devices: 117 us -> 64.1 us  [on_device(): rows_all = lax.all_gather(normed, 'tensor', axis=0, tiled=True)]
    all_gather x1 -> x0, waiting for transfers between devices: 45 us -> none  [on_device(): lax.all_gather(head_weight, 'dp', axis=0, tiled=True)]
    ppermute x0 -> x7, waiting for transfers between devices: none -> 31.7 us  [the longest x4 31.5 us: ring_gather(): lower.append(lax.ppermute(lower[-1] if lower else x, axis, pairs))]
    dot_general x0 -> x1, matrix products: none -> 12.3 us  [on_device(): jnp.dot(rows_all, ring_gather(head_weight, 'dp', 0), preferred_element_ty...]
    while x1 -> x0, matrix products: 12.2 us -> none  [by_blocks(): lax.map(one_block, (matrix_rows.reshape(block_count, 512, matrix_rows.sha...]
    unnamed x5 -> x14, local copies, waits for them, and re-layouts: 2.14 us -> 12.3 us
  transfers between devices with their start and end apart: 2 -> 8, of which waited for: 2 -> 5; matrix products, arithmetic and copies ran while one was open for 0% -> 3% of each run, Pallas kernels for 0% -> 0%
where the time goes in v1:
time: 610 us
  blocking collectives  448 us (73%)
  waiting for transfers between devices  95.8 us (16%)
  local copies, waits for them, and re-layouts  21.8 us (4%)
  between operations  14.8 us (2%)
  other arithmetic  13.1 us (2%)
  matrix products  12.3 us (2%)
    psum x1, blocking collectives, on_device(): lax.psum((totals * factor, weighted * factor, picked), 'tensor')  274 us
    pmax x1, blocking collectives, on_device(): largest = lax.pmax(highest, 'tensor')  140 us
    all_gather x1, waiting for transfers between devices, on_device(): rows_all = lax.all_gather(normed, 'tensor', axis=0, tiled=True)  64.1 us
    unnamed x1, blocking collectives  34 us
    ppermute x4, waiting for transfers between devices, ring_gather(): lower.append(lax.ppermute(lower[-1] if lower else x, axis, pairs))  31.5 us
    unnamed x14, local copies, waits for them, and re-layouts  12.3 us
    dot_general x1, matrix products, on_device(): jnp.dot(rows_all, ring_gather(head_weight, 'dp', 0), preferred_element_ty...  12.3 us
  transfers between devices with their start and end apart: 8, of which 5 were waited for; matrix products, arithmetic and copies ran while one was open for 3% of the time, Pallas kernels for 0%

profile of v1, /device:TPU:8, one launch (start us, length us, event | category | flops | bytes accessed | tf_op | source)
XLA Modules:
  0.0 609.6 jit_solution(6059714289264281289)
XLA Ops:
  7.2 1.1 fusion.5
  8.3 1.6 fusion.7
  10.0 12.0 %collective-permute-done = bf16[320,1188]{1,0:T(8,128)(2,1)S(1)} collective-permute-done((bf16[320,1188]{1,0:T(8,128)(2,1)}, bf16[320,1188]{1,0:T(8,128)(2,1)S(1)}, u32[]{:S(2)}, u32[]{:S(2)}) %collective-permute-start) | collective-permute-done | bytes 760352 | tf_op jit(solution)/shard_map/ppermute | solution.py:20
  21.9 1.7 collective-permute-start.4
  23.7 10.0 %collective-permute-done.1 = bf16[320,1188]{1,0:T(8,128)(2,1)S(1)} collective-permute-done((bf16[320,1188]{1,0:T(8,128)(2,1)S(1)}, bf16[320,1188]{1,0:T(8,128)(2,1)S(1)}, u32[]{:S(2)}, u32[]{:S(2)}) %collective-permute-start.1) | collective-permute-done | bytes 760352 | tf_op jit(solution)/shard_map/ppermute | solution.py:20
  33.9 2.2 collective-permute-start.5
  36.1 9.5 %collective-permute-done.2 = bf16[320,1188]{1,0:T(8,128)(2,1)} collective-permute-done((bf16[320,1188]{1,0:T(8,128)(2,1)S(1)}, bf16[320,1188]{1,0:T(8,128)(2,1)}, u32[]{:S(2)}, u32[]{:S(2)}) %collective-permute-start.2) | collective-permute-done | bytes 760352 | tf_op jit(solution)/shard_map/ppermute | solution.py:20
  45.6 1.3 dynamic-slice
  47.5 0.9 dynamic-update-slice
  48.4 34.0 %all-reduce = s32[1024]{0:T(1024)S(1)} all-reduce(s32[1024]{0:T(1024)S(1)} %dynamic-update-slice), channel_id=1, replica_groups=mesh['dp'=8,'tensor'=64] {'tensor'}, use_global_device_ids=true, to_apply=%add | all-reduce | flops 1024 | bytes 8192
  82.4 0.7 copy.16
  83.4 2.1 bitcast_dynamic-update-slice_fusion.7
  85.5 2.1 bitcast_dynamic-update-slice_fusion.6
  87.6 1.0 bitcast_dynamic-update-slice_fusion.5
  88.6 1.0 bitcast_dynamic-update-slice_fusion.4
  89.6 0.9 bitcast_dynamic-update-slice_fusion.3
  90.6 1.0 bitcast_dynamic-update-slice_fusion.2
  91.5 2.1 bitcast_dynamic-update-slice_fusion.1
  93.6 1.0 bitcast_dynamic-update-slice_fusion
  94.6 6.6 %gather_fusion = bf16[8,320,1188]{2,1,0:T(8,128)(2,1)} fusion(bf16[8,320,1188]{2,1,0:T(8,128)(2,1)} %bitcast_dynamic-update-slice_fusion, s32[1024]{0:T(1024)S(1)} %pad_clamp_fusion), kind=kCustom, calls=%fused_computation | custom fusion | bytes 12165152 | tf_op jit(solution)/shard_map/gather | solution.py:25
  101.2 64.1 %all-gather.2.cloned.1.call-done = bf16[1024,2560]{1,0:T(8,128)(2,1)} async-done(((bf16[16,2560]{1,0:T(8,128)(2,1)}), bf16[1024,2560]{1,0:T(8,128)(2,1)}) %all-gather.2.cloned.1.call-update) | async-done | bytes 5242896 | tf_op jit(solution)/shard_map/all_gather | solution.py:81
  165.3 12.3 %fusion.14 = f32[2,512,1188]{2,1,0:T(8,128)} fusion(bf16[2,512,2560]{2,1,0:T(8,128)(2,1)} %bitcast.83, bf16[2560,1188,1]{1,0,2:T(8,128)(2,1)} %bitcast.70), kind=kOutput, calls=%fused_computation.46 | convolution fusion | flops 6228541440 | bytes 16191488 | tf_op jit(solution)/shard_map/dot_general | solution.py:82
  177.5 9.5 %while.10 = (s32[]{:T(128)}, f32[2,4,512]{2,1,0:T(4,128)S(1)}, f32[2,512,1188]{2,1,0:T(8,128)}, s32[2,512]{1,0:T(2,128)S(1)}, s32[]{:T(128)}, /*index=5*/s32[]{:T(128)}) while((s32[]{:T(128)}, f32[2,4,512]{2,1,0:T(4,128)S(1)}, f32[2,512,1188]{2,1,0:T(8,128)}, s32[2,512]{1,0:T(2,128)S(1)}, s32[]{:T(128)}, /*index=5*/s32[]{:T(128)}) %tuple.34), condition=%wide.region_6.7_spmd, body=%wide.region_1.6_spmd.sunk | while | flops 4870658 | bytes 4898905 | solution.py:46
  177.5 1.9 dynamic-slice_reduce_fusion.2
  179.5 2.7 fusion.19
  182.3 1.9 dynamic-slice_reduce_fusion.2
  184.2 2.7 fusion.19
  187.0 139.8 %pmax.7 = f32[1024]{0:T(1024)S(1)} all-reduce(f32[1024]{0:T(1024)S(1)} %bitcast.76), channel_id=1, replica_groups=mesh['dp'=8,'tensor'=64] {'tensor'}, use_global_device_ids=true, to_apply=%region_8.9 | all-reduce | flops 1024 | bytes 8192 | tf_op jit(solution)/shard_map/pmax | solution.py:94
  326.9 274.1 %all-reduce.1 = (f32[1024]{0:T(1024)S(1)}, f32[1024]{0:T(1024)S(1)}, f32[1024]{0:T(1024)S(1)}) all-reduce(f32[1024]{0:T(1024)S(1)} %bitcast.79, f32[1024]{0:T(1024)S(1)} %get-tuple-element.69, f32[1024]{0:T(1024)S(1)} %get-tuple-element.68), channel_id=1, replica_groups=mesh['dp'=8,'tensor'=64] {'tensor'}, use_global_device_ids=true, to_apply=%region_7.8 | all-reduce | flops 3072 | bytes 24576 | tf_op jit(solution)/shard_map/psum | solution.py:96
  601.1 0.5 bitcast_divide_fusion
  601.6 0.6 dynamic_slice.14
  602.2 0.6 dynamic_slice.15
  (32 shorter events, 0.8 us)
Async XLA Ops:
  7.2 82.5 %copy-start = (bf16[320,1188]{1,0:T(8,128)(2,1)S(1)}, bf16[320,1188]{1,0:T(8,128)(2,1)}, u32[]{:S(2)}) copy-start(bf16[320,1188]{1,0:T(8,128)(2,1)} %param.9) | copy-start | bytes 2280964
  7.2 158.1 %all-gather.2.cloned.1.call-start = ((), (), s32[]{:S(2)}) async-start(), calls=%async_computation | async-start | bytes 5324800 | tf_op jit(solution)/shard_map/all_gather | solution.py:81
  9.9 12.0 %collective-permute-start = (bf16[320,1188]{1,0:T(8,128)(2,1)}, bf16[320,1188]{1,0:T(8,128)(2,1)S(1)}, u32[]{:S(2)}, u32[]{:S(2)}) collective-permute-start(bf16[320,1188]{1,0:T(8,128)(2,1)} %param.9), channel_id=1, source_target_pairs={{0,64},{64,128},{128,192},{192,256},{256,320},{320,384},{384,448},... | collective-permute-start | bytes 2280968 | tf_op jit(solution)/shard_map/ppermute | solution.py:20
  21.9 11.8 %collective-permute-start.1 = (bf16[320,1188]{1,0:T(8,128)(2,1)S(1)}, bf16[320,1188]{1,0:T(8,128)(2,1)S(1)}, u32[]{:S(2)}, u32[]{:S(2)}) collective-permute-start(bf16[320,1188]{1,0:T(8,128)(2,1)S(1)} %collective-permute-done), channel_id=1, source_target_pairs={{0,64},{64,128},{128,192},{192,256},{256,320},{320,384},{384,448},... | collective-permute-start | bytes 2280968 | tf_op jit(solution)/shard_map/ppermute | solution.py:20
  21.9 11.9 %collective-permute-start.4 = (bf16[320,1188]{1,0:T(8,128)(2,1)}, bf16[320,1188]{1,0:T(8,128)(2,1)S(1)}, u32[]{:S(2)}, u32[]{:S(2)}) collective-permute-start(bf16[320,1188]{1,0:T(8,128)(2,1)} %param.9), channel_id=1, source_target_pairs={{64,0},{128,64},{192,128},{256,192},{320,256},{384,320},{448,384},... | collective-permute-start | bytes 2280968 | tf_op jit(solution)/shard_map/ppermute | solution.py:22
  33.7 11.9 %collective-permute-start.2 = (bf16[320,1188]{1,0:T(8,128)(2,1)S(1)}, bf16[320,1188]{1,0:T(8,128)(2,1)}, u32[]{:S(2)}, u32[]{:S(2)}) collective-permute-start(bf16[320,1188]{1,0:T(8,128)(2,1)S(1)} %collective-permute-done.1), channel_id=1, source_target_pairs={{0,64},{64,128},{128,192},{192,256},{256,320},{320,384},{384,448},... | collective-permute-start | bytes 2280968 | tf_op jit(solution)/shard_map/ppermute | solution.py:20
  33.9 49.5 %collective-permute-start.5 = (bf16[320,1188]{1,0:T(8,128)(2,1)S(1)}, bf16[320,1188]{1,0:T(8,128)(2,1)}, u32[]{:S(2)}, u32[]{:S(2)}) collective-permute-start(bf16[320,1188]{1,0:T(8,128)(2,1)S(1)} %collective-permute-done.4), channel_id=1, source_target_pairs={{64,0},{128,64},{192,128},{256,192},{320,256},{384,320},{448,384},... | collective-permute-start | bytes 2280968 | tf_op jit(solution)/shard_map/ppermute | solution.py:22
  45.6 37.8 %collective-permute-start.3 = (bf16[320,1188]{1,0:T(8,128)(2,1)}, bf16[320,1188]{1,0:T(8,128)(2,1)}, u32[]{:S(2)}, u32[]{:S(2)}) collective-permute-start(bf16[320,1188]{1,0:T(8,128)(2,1)} %collective-permute-done.2), channel_id=1, source_target_pairs={{0,64},{64,128},{128,192},{192,256},{256,320},{320,384},{384,448},... | collective-permute-start | bytes 2280968 | tf_op jit(solution)/shard_map/ppermute | solution.py:20
  83.4 10.3 %collective-permute-start.6 = (bf16[320,1188]{1,0:T(8,128)(2,1)}, bf16[320,1188]{1,0:T(8,128)(2,1)S(1)}, u32[]{:S(2)}, u32[]{:S(2)}) collective-permute-start(bf16[320,1188]{1,0:T(8,128)(2,1)} %collective-permute-done.5), channel_id=1, source_target_pairs={{64,0},{128,64},{192,128},{256,192},{320,256},{384,320},{448,384},... | collective-permute-start | bytes 2280968 | tf_op jit(solution)/shard_map/ppermute | solution.py:22
  177.5 423.6 %copy-start.1 = (s32[1,16]{1,0:T(1,128)S(1)}, s32[1,16]{1,0:T(1,128)}, u32[]{:S(2)}) copy-start(s32[1,16]{1,0:T(1,128)} %param.11) | copy-start | bytes 196
Sparse Core Ops, SparseCore 0:
  11.0 154.2 all-gather.1
